TPU v7x, 512 devices: a whole 4x8x8 slice. The times are simulated.
512 devices in a mesh: rep: 32 (over y, x), tp: 16 (over z, core).
Axes of the slice: x: 4, y: 8, z: 8, core: 2. Of those that a mesh axis runs over, the one named last changes fastest.
Arguments:
- hidden: bfloat16 [147456, 4096], P('rep', 'tp'), may hold values from -0.09375 to 0.09375
- out_grad: bfloat16 [147456, 512], P(('rep', 'tp')), may hold values from -6 to 6
- momentum: float32 [32, 4096, 512], P('rep', 'tp'), may hold values from -6 to 6
- band_rows: int32 [64, 8], P('tp'), may hold values from 0 to 48, as said below
- band_start_columns: int32 [64, 8], P('tp'), may hold values from 0 to 48, as said below
Outputs:
- momentum_out: float32 [32, 4096, 512], P('rep', 'tp')
- update: bfloat16 [4096, 512], P('tp')
Inputs may be any that keep to these rules, and one draw needn't show every extreme that they name: `band_rows`: multiples of 16, the same for every replica. `band_start_columns`: multiples of 16, the same for every replica.
All inputs are finite; a program needn't handle non-finite values.
Results may differ from a plain program's by a relative error of at most 0.001.
Values may be sent and summed in bfloat16 or wider, within the bound.
A program may use at most 64 MiB of HBM per device.

v0:
```python
import jax
import jax.numpy as jnp
from jax import lax
from jax.sharding import PartitionSpec as P

decay_rate = 0.9
highest_precision = lax.Precision.HIGHEST


def band_basis(offsets):
    frequency = (offsets.reshape(-1, 1, 1) + jnp.arange(16, dtype=jnp.int32)[None, :, None]).astype(
        jnp.float32
    )
    sample_pos = jnp.arange(64, dtype=jnp.float32)[None, None, :]
    norm_scale = jnp.where(
        frequency == 0, jnp.sqrt(jnp.float32(1.0 / 64)), jnp.sqrt(jnp.float32(2.0 / 64))
    )
    return norm_scale * jnp.cos(jnp.pi * (sample_pos + 0.5) * frequency / 64)


def local(hidden, out_grad, momentum, band_rows, band_start_columns):
    row_count = hidden.shape[1]
    col_count = out_grad.shape[1]
    group_rows = row_count // 64
    group_cols = col_count // 64
    row_cosine_matrix = band_basis(band_rows)
    column_cosine_matrix = band_basis(band_start_columns)

    def from_blocks(blocks):
        return (
            blocks.reshape(group_rows, group_cols, 64, 64)
            .transpose(0, 2, 1, 3)
            .reshape(row_count, col_count)
        )

    def lift(frequency_bands):
        return jnp.einsum(
            "cji,cjk,ckl->cil",
            row_cosine_matrix,
            frequency_bands,
            column_cosine_matrix,
            precision=highest_precision,
        )

    carried_over = decay_rate * momentum[0]
    gradient = lax.dot_general(
        hidden,
        lax.all_gather(out_grad, "tp", axis=0, tiled=True),
        (((0,), (0,)), ((), ())),
        preferred_element_type=jnp.float32,
    )
    combined_blocks = (
        (carried_over + gradient)
        .reshape(group_rows, 64, group_cols, 64)
        .transpose(0, 2, 1, 3)
        .reshape(group_rows * group_cols, 64, 64)
    )
    frequency_bands = jnp.einsum(
        "hag,hgt,hbt->hab",
        row_cosine_matrix,
        combined_blocks,
        column_cosine_matrix,
        precision=highest_precision,
    )
    momentum_out = from_blocks(combined_blocks - lift(frequency_bands))
    summed = lax.psum(frequency_bands, "rep")
    update = from_blocks(lift(summed)).astype(jnp.bfloat16)
    return (momentum_out[None], update)


def solution(mesh):
    return jax.shard_map(
        local,
        mesh=mesh,
        in_specs=(
            P("rep", "tp"),
            P(("rep", "tp"), None),
            P("rep", "tp", None),
            P("tp", None),
            P("tp", None),
        ),
        out_specs=(P("rep", "tp", None), P("tp", None)),
        check_vma=False,
    )
```

profile of v0, /device:TPU:64, one launch (start us, length us, event | category | flops | bytes accessed | tf_op | source)
XLA Modules:
  0.0 236.8 jit_solution(10525231038267833556)
XLA Ops:
  7.2 0.0 copy-start
  7.2 0.0 all-gather.2.cloned.1.call-start
  7.2 0.7 all-gather.2.cloned.1.call-update
  7.9 0.8 add.63
  8.7 0.8 add.68
  9.4 0.1 compare_select_fusion
  9.5 0.1 add_convert_fusion
  9.6 0.1 compare_select_fusion.1
  9.7 0.1 add_convert_fusion.1
  9.7 49.2 %all-gather.2.cloned.1.call-done = bf16[4608,512]{1,0:T(8,128)(2,1)} async-done(((bf16[288,512]{1,0:T(8,128)(2,1)}), bf16[4608,512]{1,0:T(8,128)(2,1)}) %all-gather.2.cloned.1.call-update) | async-done | bytes 4718608 | tf_op jit(solution)/shard_map/all_gather | solution.py:48
  59.0 0.0 copy-done
  59.0 3.9 %convolution_add_fusion = f32[256,512]{1,0:T(8,128)S(1)} fusion(bf16[4608,256]{1,0:T(8,128)(2,1)S(1)} %copy-done, bf16[4608,512]{1,0:T(8,128)(2,1)} %all-gather.2.cloned.1.call-done, f32[1,256,512]{2,1,0:T(8,128)} %param.7), kind=kOutput, calls=%fused_computation.2 | convolution fusion | flops 1208221696 | bytes 8126464 | tf_op jit(solution)/shard_map/dot_general | solution.py:46
  62.9 1.2 reshape.138
  64.0 1.4 copy.7
  65.5 2.0 fusion.3
  67.5 2.2 fusion
  69.7 145.4 %psum.7 = f32[32,16,16]{2,1,0:T(8,128)} all-reduce(f32[32,16,16]{2,1,0:T(8,128)} %fusion), channel_id=1, replica_groups=mesh['rep'=32,'tp'=16] {'rep'}, use_global_device_ids=true, to_apply=%region_0.1 | all-reduce | flops 8192 | bytes 65536 | tf_op jit(solution)/shard_map/psum | solution.py:66
  215.1 2.4 %fusion.2 = f32[32,16,64]{2,1,0:T(8,128)S(1)} fusion(f32[32,16,16]{2,1,0:T(8,128)} %fusion, f32[32,16]{1,0:T(8,128)S(1)} %add_convert_fusion.1, f32[64]{0:T(128)S(1)} %add_multiply_fusion, f32[32,16]{1,0:T(8,128)S(1)} %compare_select_fusion.1), kind=kOutput, calls=%fused_computation.7 | convolution fusion | flops 6389760 | bytes 168192 | tf_op jit(solution)/shard_map/cji,cjk,ckl->cil/dot_general | solution.py:37
  217.5 2.7 %convolution_subtract_fusion = f32[32,64,64]{2,1,0:T(8,128)S(1)} fusion(f32[32,64,64]{2,1,0:T(8,128)S(1)} %bitcast.23, f32[32,16,64]{2,1,0:T(8,128)S(1)} %fusion.2, f32[32,16]{1,0:T(8,128)S(1)} %add_convert_fusion, f32[32,16]{1,0:T(8,128)S(1)} %compare_select_fusion, f32[64]{0:T(128)S(1)} %add_multiply_fusion), kind=kOutput, calls=%fused_computation | convolution fusion | flops 25395200 | bytes 1184000 | tf_op jit(solution)/shard_map/cji,cjk,ckl->cil/dot_general | solution.py:37
  220.2 3.1 %fusion.1 = f32[32,16,64]{2,1,0:T(8,128)} fusion(f32[32,16,16]{2,1,0:T(8,128)} %psum.7, f32[32,16]{1,0:T(8,128)S(1)} %add_convert_fusion.1, f32[64]{0:T(128)S(1)} %add_multiply_fusion, f32[32,16]{1,0:T(8,128)S(1)} %compare_select_fusion.1), kind=kOutput, calls=%fused_computation.6 | convolution fusion | flops 6389760 | bytes 168192 | tf_op jit(solution)/shard_map/cji,cjk,ckl->cil/dot_general | solution.py:37
  223.3 0.6 copy.8
  223.9 1.1 broadcast_in_dim_reshape.3
  225.0 3.6 %convolution_convert_fusion = bf16[32,64,64]{2,1,0:T(8,128)(2,1)S(1)} fusion(f32[32,16,64]{2,1,0:T(8,128)} %fusion.1, f32[32,16]{1,0:T(8,128)S(1)} %add_convert_fusion, f32[32,16]{1,0:T(8,128)S(1)} %compare_select_fusion, f32[64]{0:T(128)S(1)} %add_multiply_fusion), kind=kOutput, calls=%fused_computation.1 | convolution fusion | flops 25395200 | bytes 397568 | tf_op jit(solution)/shard_map/cji,cjk,ckl->cil/dot_general | solution.py:37
  228.6 0.3 copy.9
  229.0 1.0 convert_element_type.39
  (1 shorter events, 0.0 us)
Async XLA Ops:
  7.2 51.8 %copy-start = (bf16[4608,256]{1,0:T(8,128)(2,1)S(1)}, bf16[4608,256]{1,0:T(8,128)(2,1)}, u32[]{:S(2)}) copy-start(bf16[4608,256]{1,0:T(8,128)(2,1)} %param.5) | copy-start | bytes 7077892
  7.2 51.8 %all-gather.2.cloned.1.call-start = ((), (), s32[]{:S(2)}) async-start(), calls=%async_computation | async-start | bytes 5013504 | tf_op jit(solution)/shard_map/all_gather | solution.py:48
Sparse Core Ops, SparseCore 0:
  10.1 48.8 all-gather.1
where the time goes:
time: 237 us
  blocking collectives  145 us (61%)
  waiting for transfers between devices  49.9 us (21%)
  matrix products  19.8 us (8%)
  between operations  14.1 us (6%)
  local copies, waits for them, and re-layouts  7.18 us (3%)
    psum x1, blocking collectives, local(): summed = lax.psum(frequency_bands, 'rep')  145 us
    all_gather x1, waiting for transfers between devices, local(): lax.all_gather(out_grad, 'tp', axis=0, tiled=True)  49.2 us
    dot_general x4, matrix products, lift(): jnp.einsum('cji,cjk,ckl->cil', row_cosine_matrix, frequency_bands, column...  11.8 us
  transfers between devices with their start and end apart: 1, of which 1 were waited for; matrix products, arithmetic and copies ran while one was open for 1% of the time, Pallas kernels for 0%

commit v1 on v0

v1 whole, which is shorter than its diff:
```python
import functools

import jax
import jax.numpy as jnp
import numpy as np
from jax import lax
from jax.experimental import pallas as pl
from jax.experimental.pallas import tpu as pltpu
from jax.sharding import PartitionSpec as P

MESH = pl.DeviceIdType.MESH
NX = 4
NQ = 4
QW = 128
f32 = jnp.float32
bf16 = jnp.bfloat16


def block_basis():
    k = np.arange(64)[:, None].astype(np.float64)
    n = np.arange(64)[None, :].astype(np.float64)
    scale = np.where(k == 0, np.sqrt(1.0 / 64), np.sqrt(2.0 / 64))
    b = scale * np.cos(np.pi * (n + 0.5) * k / 64)
    return np.kron(np.eye(4), b).astype(np.float32)


def split(v):
    hi = v.astype(bf16)
    return hi, (v - hi.astype(f32)).astype(bf16)


def mm(a, b):
    return lax.dot_general(a, b, (((1,), (0,)), ((), ())), preferred_element_type=f32)


def mmt(a, b):
    return lax.dot_general(a, b, (((1,), (1,)), ((), ())), preferred_element_type=f32)


def mm3(dot, a, b):
    (ah, al), (bh, bl) = a, b
    return dot(ah, bh) + (dot(ah, bl) + dot(al, bh))


def kernel(
    dims, td,
    og, hid, mom, rows, cols, dmat,
    mom_out, upd_out,
    hperm, ht, o, g, rst, rt, wt, band, xbuf, xsum, ybuf, movm, updv,
    ring_s, ring_r, part_s, part_r, x_s, x_r, y_s, y_r, loc, out_s, greet,
):
    ny, nx, nz = dims
    ng = nz // 2
    rep = lax.axis_index("rep")
    tp = lax.axis_index("tp")
    y, x = rep // nx, rep % nx
    z, core = tp // 2, tp % 2
    toward = 1 - 2 * core

    def along_z(k):
        return (rep, lax.rem(z + k + nz, nz) * 2 + core)

    def along_x(k):
        return (y * nx + lax.rem(x + k + nx, nx), tp)

    def along_y(k):
        return (lax.rem(y + k + ny, ny) * nx + x, tp)

    partner = (rep, z * 2 + 1 - core)

    def local(src, dst, n):
        return pltpu.make_async_copy(src, dst, loc.at[n])

    own_o = [local(og.at[:, pl.ds(q * QW, QW)], o.at[q, ng - 1, pl.ds(0, td)], q) for q in range(NQ)]
    own_g = [local(mom.at[0, :, pl.ds(q * QW, QW)], g.at[q], NQ + q) for q in range(NQ)]
    own_h = []
    for gi in range(ng):
        for k in range(4):
            if gi < ng - 1:
                chip = z - (gi + 1) if k < 2 else z + (gi + 1)
            else:
                chip = z if k < 2 else z + nz // 2
            c = core if k % 2 == 0 else 1 - core
            t = lax.rem(chip + nz, nz) * 2 + c
            own_h.append(
                local(hid.at[pl.ds(pl.multiple_of(t * td, 32), td)], hperm.at[gi, pl.ds(k * td, td)], 2 * NQ + gi * 4 + k)
            )

    near = [along_z(1), along_z(-1), partner]
    if nx > 1:
        near += [along_x(1), along_x(-1)]
    if ny > 1:
        near += [along_y(1), along_y(-1)]
    barrier = pltpu.get_barrier_semaphore()
    for d in near:
        pl.semaphore_signal(barrier, inc=1, device_id=d, device_id_type=MESH)
    for c in own_h[:4]:
        c.start()
    for c in own_o:
        c.start()
    for c in own_g:
        c.start()
    for c in own_h[4:]:
        c.start()
    pl.semaphore_wait(barrier, len(near))

    sends = []

    def remote(src, dst, ss, rs, dev):
        return pltpu.make_async_remote_copy(
            src_ref=src, dst_ref=dst, send_sem=ss, recv_sem=rs, device_id=dev, device_id_type=MESH
        )

    def start(c):
        c.start()
        sends.append(c)

    def slot(q, gi, k):
        return o.at[q, gi, pl.ds(k * td, td)]

    def ring(q, h, side, src):
        if h < ng - 1:
            return remote(src, slot(q, h, 2 * side), ring_s.at[q, h, side], ring_r.at[q, h, side],
                          along_z(1 if side == 0 else -1))
        return remote(src, slot(q, ng - 1, 2), ring_s.at[q, h, 0], ring_r.at[q, h, 0], along_z(toward))

    def hand(q, gi, k, src):
        return remote(src, slot(q, gi, k + 1), part_s.at[q, gi, k // 2], part_r.at[q, gi, k // 2], partner)

    for q in range(NQ):
        src = og.at[:, pl.ds(q * QW, QW)]
        if ng > 1:
            start(ring(q, 0, 0, src))
            start(ring(q, 0, 1, src))
        else:
            start(ring(q, 0, 0, src))
        start(hand(q, ng - 1, 0, src))

    rounds = []
    if nx > 1:
        rounds += [(along_x, i) for i in range(nx // 2 - 1)]
    if ny > 1:
        rounds += [(along_y, i) for i in range(ny // 2 - 1)]
    for n, (axis, _) in enumerate(rounds):
        for s, k in enumerate((1, -1)):
            pl.semaphore_signal(greet.at[n, s], inc=1, device_id=axis(k), device_id_type=MESH)
        for s in range(2):
            pl.semaphore_wait(greet.at[n, s], 1)

    def turn(gi):
        for k in range(4):
            own_h[gi * 4 + k].wait()
        for j in range(4 * td // 128):
            ht[gi, :, pl.ds(j * 128, 128)] = jnp.transpose(hperm[gi, pl.ds(j * 128, 128), :])

    def pick(start_at, base, width):
        v = dmat[pl.ds(base, 16), pl.ds(0, width)]
        for t in range(1, 4):
            v = lax.select(start_at == 16 * t, dmat[pl.ds(base + 16 * t, 16), pl.ds(0, width)], v)
        return v

    def bases(q):
        wt[q] = jnp.zeros((2, 128, 512), bf16)
        for b in range(2):
            for a in range(4):
                r = pick(rows[a, 2 * q + b], 64 * a, 256)
                rh, rl = split(r)
                rst[q, 0, pl.ds(64 * b + 16 * a, 16)] = rh
                rst[q, 1, pl.ds(64 * b + 16 * a, 16)] = rl
                wh, wl = split(pick(cols[a, 2 * q + b], 64 * b, 128))
                wt[q, 0, pl.ds(32 * a + 16 * b, 16), pl.ds(128 * a, 128)] = wh
                wt[q, 1, pl.ds(32 * a + 16 * b, 16), pl.ds(128 * a, 128)] = wl
        rt[q, 0] = jnp.transpose(rst[q, 0])
        rt[q, 1] = jnp.transpose(rst[q, 1])

    def product(q, gi):
        return mm(ht[gi], o[q, gi])

    lane = lax.broadcasted_iota(jnp.int32, (64, 128), 1)

    def analyse(q):
        yst = mm3(mm, (rst[q, 0], rst[q, 1]), split(g[q]))
        yc = jnp.where(lane < 64, yst[0:64], yst[64:128])
        wide = jnp.concatenate([yc[16 * a:16 * a + 16] for a in range(4)], axis=1)
        return mm3(mmt, split(wide), (wt[q, 0], wt[q, 1]))

    def lift(q, bands):
        wide = mm3(mm, split(bands), (wt[q, 0], wt[q, 1]))
        yc = jnp.concatenate([wide[:, 128 * a:128 * a + 128] for a in range(4)], axis=0)
        stack = jnp.concatenate([jnp.where(lane < 64, yc, 0.0), jnp.where(lane < 64, 0.0, yc)], axis=0)
        return mm3(mm, (rt[q, 0], rt[q, 1]), split(stack))

    def x_copy(q, i):
        return remote(band.at[q], xbuf.at[q, x], x_s.at[q, i - 1], x_r.at[q, i - 1], along_x(i))

    def y_copy(q, i):
        return remote(xsum.at[q], ybuf.at[q, y], y_s.at[q, i - 1], y_r.at[q, i - 1], along_y(i))

    def x_send(q):
        v = analyse(q)
        band[q] = v
        for i in sorted(range(1, nx), key=lambda i: -min(i, nx - i)):
            start(x_copy(q, i))
        xbuf[q, x] = v

    def y_send(q):
        for i in range(1, nx):
            x_copy(q, i).wait_recv()
        s = xbuf[q, 0]
        for i in range(1, nx):
            s = s + xbuf[q, i]
        xsum[q] = s
        for i in sorted(range(1, ny), key=lambda i: -min(i, ny - i)):
            start(y_copy(q, i))
        ybuf[q, y] = s

    def mom_copy(q):
        return pltpu.make_async_copy(movm.at[q], mom_out.at[0, :, pl.ds(q * QW, QW)], out_s.at[q])

    def upd_copy(q):
        return pltpu.make_async_copy(updv.at[q], upd_out.at[:, pl.ds(q * QW, QW)], out_s.at[NQ + q])

    def keep(q):
        movm[q] = g[q] - lift(q, band[q])
        mom_copy(q).start()

    def finish(q):
        for i in range(1, ny):
            y_copy(q, i).wait_recv()
        s = ybuf[q, 0]
        for i in range(1, ny):
            s = s + ybuf[q, i]
        updv[q] = lift(q, s).astype(bf16)
        upd_copy(q).start()

    def arrive(q, h):
        if h < ng - 1:
            for side in range(2):
                here = slot(q, h, 2 * side)
                ring(q, h, side, here).wait_recv()
                if h + 1 < ng - 1:
                    start(ring(q, h + 1, side, here))
                start(hand(q, h, 2 * side, here))
            if h + 1 == ng - 1:
                start(ring(q, h + 1, 0, o.at[q, h, pl.ds(pl.multiple_of(core * 2 * td, 32), td)]))
        else:
            here = slot(q, h, 2)
            ring(q, h, 0, here).wait_recv()
            start(hand(q, h, 2, here))

    def gather(q, h):
        for k in (0, 2):
            hand(q, h, k, slot(q, h, k)).wait_recv()
        if h == ng - 1:
            own_o[q].wait()
        g[q] += product(q, h)

    turn(0)
    for q in range(NQ):
        own_g[q].wait()
        g[q] = 0.9 * g[q]

    extra = [functools.partial(bases, q) for q in range(NQ)]
    extra = [functools.partial(turn, gi) for gi in range(1, ng)] + extra
    prior = None
    for h in range(ng):
        for q in range(NQ):
            arrive(q, h)
            last = h == ng - 1 and q == 0
            while extra and (last or len(extra) > 0):
                extra.pop(0)()
                if not last:
                    break
            if prior is not None:
                gather(*prior)
                if prior[1] == ng - 1:
                    x_send(prior[0])
                    if prior[0] >= 2:
                        y_send(prior[0] - 2)
            prior = (q, h)
    gather(*prior)
    x_send(NQ - 1)
    y_send(NQ - 3)
    y_send(NQ - 2)
    keep(0)
    y_send(NQ - 1)
    for q in range(1, NQ):
        keep(q)
    for q in range(NQ):
        finish(q)
    for c in sends:
        c.wait_send()
    for q in range(NQ):
        mom_copy(q).wait()
        upd_copy(q).wait()


def build(dims, td):
    ny, nx, nz = dims
    ng = nz // 2
    dma = pltpu.SemaphoreType.DMA
    n_greet = max(1, (nx // 2 - 1 if nx > 1 else 0) + (ny // 2 - 1 if ny > 1 else 0))
    anyspace = pl.BlockSpec(memory_space=pl.ANY)
    return pl.pallas_call(
        functools.partial(kernel, dims, td),
        name="demo_step",
        out_shape=(
            jax.ShapeDtypeStruct((1, 256, 512), f32),
            jax.ShapeDtypeStruct((256, 512), bf16),
        ),
        in_specs=[
            anyspace, anyspace, anyspace,
            pl.BlockSpec(memory_space=pltpu.SMEM),
            pl.BlockSpec(memory_space=pltpu.SMEM),
            pl.BlockSpec(memory_space=pltpu.VMEM),
        ],
        out_specs=(anyspace, anyspace),
        scratch_shapes=[
            pltpu.VMEM((ng, 4 * td, 256), bf16),
            pltpu.VMEM((ng, 256, 4 * td), bf16),
            pltpu.VMEM((NQ, ng, 4 * td, QW), bf16),
            pltpu.VMEM((NQ, 256, QW), f32),
            pltpu.VMEM((NQ, 2, 128, 256), bf16),
            pltpu.VMEM((NQ, 2, 256, 128), bf16),
            pltpu.VMEM((NQ, 2, 128, 512), bf16),
            pltpu.VMEM((NQ, 16, 128), f32),
            pltpu.VMEM((NQ, nx, 16, 128), f32),
            pltpu.VMEM((NQ, 16, 128), f32),
            pltpu.VMEM((NQ, ny, 16, 128), f32),
            pltpu.VMEM((NQ, 256, QW), f32),
            pltpu.VMEM((NQ, 256, QW), bf16),
            dma((NQ, ng, 2)), dma((NQ, ng, 2)),
            dma((NQ, ng, 2)), dma((NQ, ng, 2)),
            dma((NQ, max(nx - 1, 1))), dma((NQ, max(nx - 1, 1))),
            dma((NQ, max(ny - 1, 1))), dma((NQ, max(ny - 1, 1))),
            dma((2 * NQ + 4 * ng,)),
            dma((2 * NQ,)),
            pltpu.SemaphoreType.REGULAR((n_greet, 2)),
        ],
        compiler_params=pltpu.CompilerParams(collective_id=0, has_side_effects=True),
    )


def solution(mesh):
    n_rep, n_tp = mesh.shape["rep"], mesh.shape["tp"]
    dims = (n_rep // NX, NX, n_tp // 2)

    def local(hidden, out_grad, momentum, band_rows, band_start_columns):
        call = build(dims, out_grad.shape[0])
        return call(out_grad, hidden, momentum, band_rows, band_start_columns, jnp.asarray(block_basis()))

    return jax.shard_map(
        local,
        mesh=mesh,
        in_specs=(
            P("rep", "tp"),
            P(("rep", "tp"), None),
            P("rep", "tp", None),
            P("tp", None),
            P("tp", None),
        ),
        out_specs=(P("rep", "tp", None), P("tp", None)),
        check_vma=False,
    )
```

time: 237 us -> 59.1 us (0.25)
  the two profiles are of different devices: /device:TPU:64 before, /device:TPU:1 now
where the time goes in v1:
time: 59.1 us; the launch traced here: 58.9 us
  Pallas kernels  54.7 us (93%)
  local copies, waits for them, and re-layouts  3.54 us (6%)
  between operations  0.64 us (1%)
    pallas_call x1, Pallas kernels, local(): call(out_grad, hidden, momentum, band_rows, band_start_columns, jnp.asarr...  54.7 us
    unnamed x2, local copies, waits for them, and re-layouts  3.54 us

profile of v1, /device:TPU:1, one launch (start us, length us, event | category | flops | bytes accessed | tf_op | source)
XLA Modules:
  0.0 58.9 jit_solution(12381898824272452400)
XLA Ops:
  0.6 54.7 %demo_step.1 = (f32[1,256,512]{2,1,0:T(8,128)}, bf16[256,512]{1,0:T(8,128)(2,1)}) custom-call(bf16[288,512]{1,0:T(8,128)(2,1)} %og.1, bf16[4608,256]{1,0:T(8,128)(2,1)} %hid.1, f32[1,256,512]{2,1,0:T(8,128)} %mom.1, s32[4,8]{1,0:T(4,128)} %rows.1, s32[4,8]{1,0:T(4,128)} %cols.1, f32[256,256]{1,0:T(8,128)} %constant.2.clone.dmat), custom_call_target="tpu_custom_call" | custom-call | tf_op jit(solution)/shard_map/demo_step/pallas_call | solution.py:350
  55.3 1.9 %copy.10 = f32[1,256,512]{2,1,0:T(8,128)} copy(f32[1,256,512]{2,1,0:T(8,128)} %get-tuple-element.4) | data formatting | bytes 1048576
  57.2 1.7 %copy.11 = bf16[256,512]{1,0:T(8,128)(2,1)} copy(bf16[256,512]{1,0:T(8,128)(2,1)} %get-tuple-element.5) | data formatting | bytes 524288

commit v2 on v1

v2 whole, which is shorter than its diff:
```python
import functools

import jax
import jax.numpy as jnp
import numpy as np
from jax import lax
from jax.experimental import pallas as pl
from jax.experimental.pallas import tpu as pltpu
from jax.sharding import PartitionSpec as P

MESH = pl.DeviceIdType.MESH
NX = 4
NQ = 4
QW = 128
f32 = jnp.float32
bf16 = jnp.bfloat16


def block_basis():
    k = np.arange(64)[:, None].astype(np.float64)
    n = np.arange(64)[None, :].astype(np.float64)
    scale = np.where(k == 0, np.sqrt(1.0 / 64), np.sqrt(2.0 / 64))
    b = scale * np.cos(np.pi * (n + 0.5) * k / 64)
    return np.kron(np.eye(4), b).astype(np.float32)


def split(v):
    hi = v.astype(bf16)
    return hi, (v - hi.astype(f32)).astype(bf16)


def mm(a, b):
    return lax.dot_general(a, b, (((1,), (0,)), ((), ())), preferred_element_type=f32)


def mmt(a, b):
    return lax.dot_general(a, b, (((1,), (1,)), ((), ())), preferred_element_type=f32)


def mm3(dot, a, b):
    (ah, al), (bh, bl) = a, b
    return dot(ah, bh) + (dot(ah, bl) + dot(al, bh))


def kernel(
    dims, td,
    og, hid, mom, rows_any, cols_any, dmat_any,
    mom_out, upd_out,
    hperm, ht, o, g, rst, rt, wt, rh, yp, band, xbuf, xsum, ybuf, movm, updv, dmat, rows, cols,
    send_s, ring_r, part_r, x_r, y_r, loc, greet,
):
    ny, nx, nz = dims
    ng = nz // 2
    rep = lax.axis_index("rep")
    tp = lax.axis_index("tp")
    y, x = rep // nx, rep % nx
    z, core = tp // 2, tp % 2

    def from_right(chip):
        return jnp.logical_or(core == 1, lax.rem(chip + nz, nz) < nz // 8)

    go_right = jnp.logical_not(from_right(z + 1))
    go_left = from_right(z - 1)

    def along_z(k):
        return (rep, lax.rem(z + k + nz, nz) * 2 + core)

    def along_x(k):
        return (y * nx + lax.rem(x + k + nx, nx), tp)

    def along_y(k):
        return (lax.rem(y + k + ny, ny) * nx + x, tp)

    partner = (rep, z * 2 + 1 - core)

    def local(src, dst, n):
        return pltpu.make_async_copy(src, dst, loc.at[n])

    consts = [local(dmat_any, dmat, 0), local(rows_any, rows, 1), local(cols_any, cols, 2)]
    own_o = [local(og.at[:, pl.ds(q * QW, QW)], o.at[q, ng - 1, pl.ds(0, td)], 3) for q in range(NQ)]
    own_g = [local(mom.at[0, :, pl.ds(q * QW, QW)], g.at[q], 4) for q in range(NQ)]
    own_h = []
    for gi in range(ng):
        for k in range(4):
            if gi < ng - 1:
                chip = z - (gi + 1) if k % 2 == 0 else z + (gi + 1)
            else:
                chip = z if k % 2 == 0 else z + nz // 2
            c = core if k < 2 else 1 - core
            t = lax.rem(chip + nz, nz) * 2 + c
            own_h.append(
                local(hid.at[pl.ds(pl.multiple_of(t * td, 32), td)], hperm.at[gi, pl.ds(k * td, td)], 7 + gi)
            )

    def drain(view, sem):
        pltpu.make_async_copy(view, view, sem).wait()

    near = [along_z(1), along_z(-1), partner]
    if nx > 1:
        near += [along_x(1), along_x(-1)]
    if ny > 1:
        near += [along_y(1), along_y(-1)]
    barrier = pltpu.get_barrier_semaphore()
    for d in near:
        pl.semaphore_signal(barrier, inc=1, device_id=d, device_id_type=MESH)
    pl.semaphore_wait(barrier, len(near))

    def remote(src, dst, ss, rs, dev):
        return pltpu.make_async_remote_copy(
            src_ref=src, dst_ref=dst, send_sem=ss, recv_sem=rs, device_id=dev, device_id_type=MESH
        )

    def slot(q, gi, k):
        return o.at[q, gi, pl.ds(k * td, td)]

    def ring(q, h, side, src):
        return remote(src, slot(q, h, side), send_s.at[0], ring_r.at[q, 2 * h + side], along_z(1 - 2 * side))

    def far(q, side, src):
        return remote(src, slot(q, ng - 1, 1), send_s.at[1 + side], ring_r.at[q, 2 * ng - 2], along_z(1 - 2 * side))

    def hand(q, gi, k, src):
        return remote(src, slot(q, gi, k + 2), send_s.at[3], part_r.at[q, gi], partner)

    def send_far(q, sources):
        for side, go in enumerate((go_right, go_left)):
            @pl.when(go)
            def _(side=side):
                far(q, side, sources[side]).start()

    for q in range(NQ):
        src = og.at[:, pl.ds(q * QW, QW)]
        if ng > 1:
            ring(q, 0, 0, src).start()
            ring(q, 0, 1, src).start()
        else:
            send_far(q, (src, src))
        hand(q, ng - 1, 0, src).start()

    for c in consts + own_h[:4] + own_g + own_o + own_h[4:]:
        c.start()

    rounds = []
    if nx > 1:
        rounds += [(along_x, i) for i in range(nx // 2 - 1)]
    if ny > 1:
        rounds += [(along_y, i) for i in range(ny // 2 - 1)]
    for n, (axis, _) in enumerate(rounds):
        for k in (1, -1):
            pl.semaphore_signal(greet.at[n], inc=1, device_id=axis(k), device_id_type=MESH)
        pl.semaphore_wait(greet.at[n], 2)

    def turn(gi):
        drain(hperm.at[gi], loc.at[7 + gi])
        for j in range(4 * td // 128):
            ht[gi, :, pl.ds(j * 128, 128)] = jnp.transpose(hperm[gi, pl.ds(j * 128, 128), :])

    def pick(start_at, base, width):
        v = dmat[pl.ds(base, 16), pl.ds(0, width)]
        for t in range(1, 4):
            v = lax.select(start_at == 16 * t, dmat[pl.ds(base + 16 * t, 16), pl.ds(0, width)], v)
        return v

    def bases(q):
        wt[q] = jnp.zeros((2, 128, 512), bf16)
        for b in range(2):
            for a in range(4):
                r = pick(rows[a, 2 * q + b], 64 * a, 256)
                hi, lo = split(r)
                rst[q, 0, pl.ds(64 * b + 16 * a, 16)] = hi
                rst[q, 1, pl.ds(64 * b + 16 * a, 16)] = lo
                wh, wl = split(pick(cols[a, 2 * q + b], 64 * b, 128))
                wt[q, 0, pl.ds(32 * a + 16 * b, 16), pl.ds(128 * a, 128)] = wh
                wt[q, 1, pl.ds(32 * a + 16 * b, 16), pl.ds(128 * a, 128)] = wl
        rt[q, 0] = jnp.transpose(rst[q, 0])
        rt[q, 1] = jnp.transpose(rst[q, 1])
        v = mm(rst[q, 0], ht[ng - 1]) + mm(rst[q, 1], ht[ng - 1])
        rh[q, 0], rh[q, 1] = split(v)

    def product(q, gi):
        return mm(ht[gi], o[q, gi])

    lane = lax.broadcasted_iota(jnp.int32, (64, 128), 1)

    def partial(q):
        yp[q] = mm3(mm, (rst[q, 0], rst[q, 1]), split(g[q]))

    def analyse(q):
        last = o[q, ng - 1]
        yst = yp[q] + (mm(rh[q, 0], last) + mm(rh[q, 1], last))
        yc = jnp.where(lane < 64, yst[0:64], yst[64:128])
        wide = jnp.concatenate([yc[16 * a:16 * a + 16] for a in range(4)], axis=1)
        return mm3(mmt, split(wide), (wt[q, 0], wt[q, 1]))

    def lift(q, bands):
        wide = mm3(mm, split(bands), (wt[q, 0], wt[q, 1]))
        yc = jnp.concatenate([wide[:, 128 * a:128 * a + 128] for a in range(4)], axis=0)
        stack = jnp.concatenate([jnp.where(lane < 64, yc, 0.0), jnp.where(lane < 64, 0.0, yc)], axis=0)
        return mm3(mm, (rt[q, 0], rt[q, 1]), split(stack))

    def x_copy(q, i):
        return remote(band.at[q], xbuf.at[q, x], send_s.at[4], x_r.at[q], along_x(i))

    def y_copy(q, i):
        return remote(xsum.at[q], ybuf.at[q, y], send_s.at[5], y_r.at[q], along_y(i))

    def x_send(q):
        v = analyse(q)
        band[q] = v
        for i in sorted(range(1, nx), key=lambda i: -min(i, nx - i)):
            x_copy(q, i).start()
        xbuf[q, x] = v

    def y_send(q):
        if nx > 1:
            drain(xbuf.at[q, pl.ds(0, nx - 1)], x_r.at[q])
        s = xbuf[q, 0]
        for i in range(1, nx):
            s = s + xbuf[q, i]
        xsum[q] = s
        for i in sorted(range(1, ny), key=lambda i: -min(i, ny - i)):
            y_copy(q, i).start()
        ybuf[q, y] = s

    def mom_copy(q):
        return pltpu.make_async_copy(movm.at[q], mom_out.at[q], loc.at[5])

    def upd_copy(q):
        return pltpu.make_async_copy(updv.at[q], upd_out.at[q], loc.at[6])

    def keep(q):
        movm[q] = g[q] + product(q, ng - 1) - lift(q, band[q])
        mom_copy(q).start()

    def finish(q):
        if ny > 1:
            drain(ybuf.at[q, pl.ds(0, ny - 1)], y_r.at[q])
        s = ybuf[q, 0]
        for i in range(1, ny):
            s = s + ybuf[q, i]
        updv[q] = lift(q, s).astype(bf16)
        upd_copy(q).start()

    def arrive(q, h):
        if h < ng - 1:
            for side in range(2):
                here = slot(q, h, side)
                ring(q, h, side, here).wait_recv()
                if h + 1 < ng - 1:
                    ring(q, h + 1, side, here).start()
                hand(q, h, side, here).start()
            if h + 1 == ng - 1:
                send_far(q, (slot(q, h, 0), slot(q, h, 1)))
        else:
            here = slot(q, h, 1)
            far(q, 0, here).wait_recv()
            hand(q, h, 1, here).start()

    def gather(q, h):
        drain(o.at[q, h, pl.ds(2 * td, 2 * td)], part_r.at[q, h])
        if h < ng - 1:
            g[q] += product(q, h)
            if h == ng - 2:
                partial(q)

    for c in consts:
        c.wait()
    turn(0)
    drain(g, loc.at[4])
    for q in range(NQ):
        g[q] = 0.9 * g[q]
        if ng == 1:
            bases(q)
            partial(q)
    drain(o.at[:, ng - 1, pl.ds(0, td)], loc.at[3])

    extra = [functools.partial(turn, gi) for gi in range(1, ng)]
    if ng > 1:
        extra += [functools.partial(bases, q) for q in range(NQ)]
    prior = None
    for h in range(ng):
        for q in range(NQ):
            arrive(q, h)
            if extra and (h or ng == 1):
                extra.pop(0)()
                if ng < 4:
                    while extra:
                        extra.pop(0)()
            if prior is not None:
                gather(*prior)
                if prior[1] == ng - 1:
                    x_send(prior[0])
                    if prior[0] >= 2:
                        y_send(prior[0] - 2)
            prior = (q, h)
    gather(*prior)
    x_send(NQ - 1)
    y_send(NQ - 3)
    y_send(NQ - 2)
    keep(0)
    y_send(NQ - 1)
    for q in range(1, NQ):
        keep(q)
    for q in range(NQ):
        finish(q)
    if ng > 1:
        drain(o.at[:, pl.ds(0, ng - 1), pl.ds(0, 2 * td)], send_s.at[0])
    for side, go in enumerate((go_right, go_left)):
        @pl.when(go)
        def _(side=side):
            drain(o.at[:, ng - 1, pl.ds(0, td)], send_s.at[1 + side])
    drain(o.at[:, :, pl.ds(0, 2 * td)], send_s.at[3])
    if nx > 1:
        drain(xbuf.at[:, pl.ds(0, nx - 1)], send_s.at[4])
    if ny > 1:
        drain(ybuf.at[:, pl.ds(0, ny - 1)], send_s.at[5])
    drain(movm, loc.at[5])
    drain(updv, loc.at[6])


def out_kernel(mom_in, upd_in, mom_out, upd_out, sems):
    def copies(q):
        return (
            pltpu.make_async_copy(mom_in.at[q], mom_out.at[0, :, pl.ds(q * QW, QW)], sems.at[0, q]),
            pltpu.make_async_copy(upd_in.at[q], upd_out.at[:, pl.ds(q * QW, QW)], sems.at[1, q]),
        )

    for q in range(NQ):
        for c in copies(q):
            c.start()
    for q in range(NQ):
        for c in copies(q):
            c.wait()


def build(dims, td):
    ny, nx, nz = dims
    ng = nz // 2
    dma = pltpu.SemaphoreType.DMA
    n_greet = max(1, (nx // 2 - 1 if nx > 1 else 0) + (ny // 2 - 1 if ny > 1 else 0))
    anyspace = pl.BlockSpec(memory_space=pl.ANY)
    hbm = pl.BlockSpec(memory_space=pltpu.HBM)
    step = pl.pallas_call(
        functools.partial(kernel, dims, td),
        name="demo_step",
        out_shape=(
            jax.ShapeDtypeStruct((NQ, 256, QW), f32),
            jax.ShapeDtypeStruct((NQ, 256, QW), bf16),
        ),
        in_specs=[hbm] * 6,
        out_specs=(anyspace, anyspace),
        scratch_shapes=[
            pltpu.VMEM((ng, 4 * td, 256), bf16),
            pltpu.VMEM((ng, 256, 4 * td), bf16),
            pltpu.VMEM((NQ, ng, 4 * td, QW), bf16),
            pltpu.VMEM((NQ, 256, QW), f32),
            pltpu.VMEM((NQ, 2, 128, 256), bf16),
            pltpu.VMEM((NQ, 2, 256, 128), bf16),
            pltpu.VMEM((NQ, 2, 128, 512), bf16),
            pltpu.VMEM((NQ, 2, 128, 4 * td), bf16),
            pltpu.VMEM((NQ, 128, 128), f32),
            pltpu.VMEM((NQ, 16, 128), f32),
            pltpu.VMEM((NQ, nx, 16, 128), f32),
            pltpu.VMEM((NQ, 16, 128), f32),
            pltpu.VMEM((NQ, ny, 16, 128), f32),
            pltpu.VMEM((NQ, 256, QW), f32),
            pltpu.VMEM((NQ, 256, QW), bf16),
            pltpu.VMEM((256, 256), f32),
            pltpu.SMEM((4, 8), jnp.int32),
            pltpu.SMEM((4, 8), jnp.int32),
            dma((6,)),
            dma((NQ, 2 * ng - 1)),
            dma((NQ, ng)),
            dma((NQ,)),
            dma((NQ,)),
            dma((7 + ng,)),
            pltpu.SemaphoreType.REGULAR((n_greet,)),
        ],
        compiler_params=pltpu.CompilerParams(
            collective_id=0, has_side_effects=True, vmem_limit_bytes=28 * 2**20
        ),
    )
    out = pl.pallas_call(
        out_kernel,
        name="results_out",
        out_shape=(
            jax.ShapeDtypeStruct((1, 256, 512), f32),
            jax.ShapeDtypeStruct((256, 512), bf16),
        ),
        in_specs=[anyspace, anyspace],
        out_specs=(anyspace, anyspace),
        scratch_shapes=[dma((2, NQ))],
        compiler_params=pltpu.CompilerParams(vmem_limit_bytes=2**20),
    )
    return lambda *args: out(*step(*[pltpu.with_memory_space_constraint(a, pltpu.HBM) for a in args]))


def solution(mesh):
    n_rep, n_tp = mesh.shape["rep"], mesh.shape["tp"]
    dims = (n_rep // NX, NX, n_tp // 2)

    def local(hidden, out_grad, momentum, band_rows, band_start_columns):
        call = build(dims, out_grad.shape[0])
        return call(out_grad, hidden, momentum, band_rows, band_start_columns, jnp.asarray(block_basis()))

    return jax.shard_map(
        local,
        mesh=mesh,
        in_specs=(
            P("rep", "tp"),
            P(("rep", "tp"), None),
            P("rep", "tp", None),
            P("tp", None),
            P("tp", None),
        ),
        out_specs=(P("rep", "tp", None), P("tp", None)),
        check_vma=False,
    )
```

time: 59.1 us -> 51.7 us (0.87)
  Pallas kernels: 54.7 us -> 50.9 us
  local copies, waits for them, and re-layouts: 3.54 us -> 0 us
    pallas_call x1 -> x2, Pallas kernels: 54.7 us -> 50.9 us  [the longest x1 50 us: build(): step(*[pltpu.with_memory_space_constraint(a, pltpu.HBM) for a in args])]
    unnamed x2 -> x0, local copies, waits for them, and re-layouts: 3.54 us -> none
where the time goes in v2:
time: 51.7 us; the launch traced here: 51.6 us
  Pallas kernels  50.9 us (98%)
  between operations  0.64 us (1%)
    pallas_call x1, Pallas kernels, build(): step(*[pltpu.with_memory_space_constraint(a, pltpu.HBM) for a in args])  50 us

profile of v2, /device:TPU:1, one launch (start us, length us, event | category | flops | bytes accessed | tf_op | source)
XLA Modules:
  0.0 51.6 jit_solution(6384018076125978107)
XLA Ops:
  0.6 50.0 %demo_step.1 = (f32[4,256,128]{2,1,0:T(8,128)S(1)}, bf16[4,256,128]{2,1,0:T(8,128)(2,1)S(1)}) custom-call(bf16[288,512]{1,0:T(8,128)(2,1)} %og.1, bf16[4608,256]{1,0:T(8,128)(2,1)} %hid.1, f32[1,256,512]{2,1,0:T(8,128)} %mom.1, s32[4,8]{1,0:T(4,128)} %rows_any.1, s32[4,8]{1,0:T(4,128)} %cols_any.1, f32[256,256]{1,0:T(8,128)} %constant.2.clone.dmat_any), custom_call_target="tpu_custom_call" | custom-call | tf_op jit(solution)/shard_map/demo_step/pallas_call | solution.py:395
  50.6 0.9 %results_out.1 = (f32[1,256,512]{2,1,0:T(8,128)}, bf16[256,512]{1,0:T(8,128)(2,1)}) custom-call(f32[4,256,128]{2,1,0:T(8,128)S(1)} %get-tuple-element.4.mom_in, bf16[4,256,128]{2,1,0:T(8,128)(2,1)S(1)} %get-tuple-element.5.upd_in), custom_call_target="tpu_custom_call" | custom-call | tf_op jit(solution)/shard_map/results_out/pallas_call | solution.py:395

commit v3 on v2

--- a/solution.py
+++ b/solution.py
@@ -12,6 +12,9 @@
 NX = 4
 NQ = 4
 QW = 128
+Y_FIRST = (0, 1)
+SECOND = (2, 3, 0, 1)
+LAST = (0, 1, 2, 3)
 f32 = jnp.float32
 bf16 = jnp.bfloat16
 
@@ -46,7 +49,7 @@
     dims, td,
     og, hid, mom, rows_any, cols_any, dmat_any,
     mom_out, upd_out,
-    hperm, ht, o, g, rst, rt, wt, rh, yp, band, xbuf, xsum, ybuf, movm, updv, dmat, rows, cols,
+    hperm, ht, o, g, rst, rt, wk, wr, rh, yp, band, xbuf, xsum, ybuf, dmat, rows, cols,
     send_s, ring_r, part_r, x_r, y_r, loc, greet,
 ):
     ny, nx, nz = dims
@@ -77,6 +80,13 @@
         return pltpu.make_async_copy(src, dst, loc.at[n])
 
     consts = [local(dmat_any, dmat, 0), local(rows_any, rows, 1), local(cols_any, cols, 2)]
+    pad = -2 * td % 128
+
+    def place(gi, k):
+        if gi < ng - 1:
+            return k * td
+        return (0, 2 * td + pad, td, 3 * td + pad)[k]
+
     own_o = [local(og.at[:, pl.ds(q * QW, QW)], o.at[q, ng - 1, pl.ds(0, td)], 3) for q in range(NQ)]
     own_g = [local(mom.at[0, :, pl.ds(q * QW, QW)], g.at[q], 4) for q in range(NQ)]
     own_h = []
@@ -89,7 +99,7 @@
             c = core if k < 2 else 1 - core
             t = lax.rem(chip + nz, nz) * 2 + c
             own_h.append(
-                local(hid.at[pl.ds(pl.multiple_of(t * td, 32), td)], hperm.at[gi, pl.ds(k * td, td)], 7 + gi)
+                local(hid.at[pl.ds(pl.multiple_of(t * td, 32), td)], hperm.at[gi, pl.ds(place(gi, k), td)], 5 + gi)
             )
 
     def drain(view, sem):
@@ -111,7 +121,7 @@
         )
 
     def slot(q, gi, k):
-        return o.at[q, gi, pl.ds(k * td, td)]
+        return o.at[q, gi, pl.ds(place(gi, k), td)]
 
     def ring(q, h, side, src):
         return remote(src, slot(q, h, side), send_s.at[0], ring_r.at[q, 2 * h + side], along_z(1 - 2 * side))
@@ -120,7 +130,8 @@
         return remote(src, slot(q, ng - 1, 1), send_s.at[1 + side], ring_r.at[q, 2 * ng - 2], along_z(1 - 2 * side))
 
     def hand(q, gi, k, src):
-        return remote(src, slot(q, gi, k + 2), send_s.at[3], part_r.at[q, gi], partner)
+        own = gi == ng - 1 and k == 0
+        return remote(src, slot(q, gi, k + 2), send_s.at[3], loc.at[5 + ng + q] if own else part_r.at[q, gi], partner)
 
     def send_far(q, sources):
         for side, go in enumerate((go_right, go_left)):
@@ -151,8 +162,8 @@
         pl.semaphore_wait(greet.at[n], 2)
 
     def turn(gi):
-        drain(hperm.at[gi], loc.at[7 + gi])
-        for j in range(4 * td // 128):
+        drain(hperm.at[gi, pl.ds(0, 4 * td)], loc.at[5 + gi])
+        for j in range((4 * td if gi < ng - 1 else 4 * td + 2 * pad) // 128):
             ht[gi, :, pl.ds(j * 128, 128)] = jnp.transpose(hperm[gi, pl.ds(j * 128, 128), :])
 
     def pick(start_at, base, width):
@@ -162,84 +173,98 @@
         return v
 
     def bases(q):
-        wt[q] = jnp.zeros((2, 128, 512), bf16)
         for b in range(2):
             for a in range(4):
-                r = pick(rows[a, 2 * q + b], 64 * a, 256)
-                hi, lo = split(r)
+                hi, lo = split(pick(rows[a, 2 * q + b], 64 * a, 256))
                 rst[q, 0, pl.ds(64 * b + 16 * a, 16)] = hi
                 rst[q, 1, pl.ds(64 * b + 16 * a, 16)] = lo
-                wh, wl = split(pick(cols[a, 2 * q + b], 64 * b, 128))
-                wt[q, 0, pl.ds(32 * a + 16 * b, 16), pl.ds(128 * a, 128)] = wh
-                wt[q, 1, pl.ds(32 * a + 16 * b, 16), pl.ds(128 * a, 128)] = wl
-        rt[q, 0] = jnp.transpose(rst[q, 0])
-        rt[q, 1] = jnp.transpose(rst[q, 1])
-        v = mm(rst[q, 0], ht[ng - 1]) + mm(rst[q, 1], ht[ng - 1])
-        rh[q, 0], rh[q, 1] = split(v)
-
-    def product(q, gi):
-        return mm(ht[gi], o[q, gi])
+                hi, lo = split(pick(cols[a, 2 * q + b], 64 * b, 128))
+                for n, v in enumerate((hi, hi, lo)):
+                    at = 32 * a + 16 * b
+                    wk[q, pl.ds(at, 16), pl.ds(128 * n, 128)] = v
+                    wr[q, pl.ds(128 * n + at, 16)] = v
+        hi, lo = jnp.transpose(rst[q, 0]), jnp.transpose(rst[q, 1])
+        for n, v in enumerate((hi, lo, hi)):
+            rt[q, :, pl.ds(128 * n, 128)] = v
+        far_h = ht[ng - 1, :, pl.ds(2 * td + pad, 2 * td)]
+        hi, lo = split(mm(rst[q, 0], far_h) + mm(rst[q, 1], far_h))
+        rh[q, pl.ds(0, 128)] = hi
+        rh[q, pl.ds(128, 128)] = lo
 
     lane = lax.broadcasted_iota(jnp.int32, (64, 128), 1)
+    lane16 = lax.broadcasted_iota(jnp.int32, (16, 128), 1)
+
+    def of_row(a, v):
+        return jnp.where(jnp.logical_and(lane16 >= 32 * a, lane16 < 32 * a + 32), v, 0.0)
+
+    def near_part(q):
+        g[q] += mm(ht[ng - 1, :, pl.ds(0, 2 * td)], o[q, ng - 1, pl.ds(0, 2 * td)])
+
+    def far_part(q):
+        far_h = ht[ng - 1, :, pl.ds(2 * td + pad, 2 * td)]
+        return mm(far_h, o[q, ng - 1, pl.ds(2 * td + pad, 2 * td)])
 
     def partial(q):
         yp[q] = mm3(mm, (rst[q, 0], rst[q, 1]), split(g[q]))
 
     def analyse(q):
-        last = o[q, ng - 1]
-        yst = yp[q] + (mm(rh[q, 0], last) + mm(rh[q, 1], last))
-        yc = jnp.where(lane < 64, yst[0:64], yst[64:128])
-        wide = jnp.concatenate([yc[16 * a:16 * a + 16] for a in range(4)], axis=1)
-        return mm3(mmt, split(wide), (wt[q, 0], wt[q, 1]))
+        v = mm(rh[q], o[q, ng - 1, pl.ds(2 * td + pad, 2 * td)])
+        yst = yp[q] + (v[0:128] + v[128:256])
+        hi, lo = split(jnp.where(lane < 64, yst[0:64], yst[64:128]))
+        v = mmt(jnp.concatenate([hi, lo, hi], axis=1), wk[q])
+        return sum(of_row(a, v[16 * a:16 * a + 16]) for a in range(1, 4)) + of_row(0, v[0:16])
 
     def lift(q, bands):
-        wide = mm3(mm, split(bands), (wt[q, 0], wt[q, 1]))
-        yc = jnp.concatenate([wide[:, 128 * a:128 * a + 128] for a in range(4)], axis=0)
-        stack = jnp.concatenate([jnp.where(lane < 64, yc, 0.0), jnp.where(lane < 64, 0.0, yc)], axis=0)
-        return mm3(mm, (rt[q, 0], rt[q, 1]), split(stack))
-
-    def x_copy(q, i):
-        return remote(band.at[q], xbuf.at[q, x], send_s.at[4], x_r.at[q], along_x(i))
-
-    def y_copy(q, i):
-        return remote(xsum.at[q], ybuf.at[q, y], send_s.at[5], y_r.at[q], along_y(i))
-
-    def x_send(q):
+        hi, lo = split(jnp.concatenate([of_row(a, bands) for a in range(4)], axis=0))
+        v = mm(jnp.concatenate([hi, lo, hi], axis=1), wr[q])
+        v = jnp.concatenate([jnp.where(lane < 64, v, 0.0), jnp.where(lane < 64, 0.0, v)], axis=0)
+        hi, lo = split(v)
+        return mm(rt[q], jnp.concatenate([hi, hi, lo], axis=0))
+
+    def axis(q, phase):
+        return "y" if (q in Y_FIRST) == (phase == 0) else "x"
+
+    def peer(name, i):
+        return along_x(i) if name == "x" else along_y(i)
+
+    size = {"x": nx, "y": ny}
+    inbox = {"x": xbuf, "y": ybuf}
+    place_of = {"x": x, "y": y}
+    arrived = {"x": x_r, "y": y_r}
+    sent = {"x": send_s.at[4], "y": send_s.at[5]}
+
+    def spread(q, phase, src, value):
+        name = axis(q, phase)
+        n = size[name]
+        for i in sorted(range(1, n), key=lambda i: -min(i, n - i)):
+            remote(src.at[q], inbox[name].at[q, place_of[name]], sent[name], arrived[name].at[q], peer(name, i)).start()
+        inbox[name][q, place_of[name]] = value
+
+    def collect(q, phase):
+        name = axis(q, phase)
+        n, buf = size[name], inbox[name]
+        if n > 1:
+            drain(buf.at[q, pl.ds(0, n - 1)], arrived[name].at[q])
+        s = buf[q, 0]
+        for i in range(1, n):
+            s = s + buf[q, i]
+        return s
+
+    def first_phase(q):
         v = analyse(q)
         band[q] = v
-        for i in sorted(range(1, nx), key=lambda i: -min(i, nx - i)):
-            x_copy(q, i).start()
-        xbuf[q, x] = v
-
-    def y_send(q):
-        if nx > 1:
-            drain(xbuf.at[q, pl.ds(0, nx - 1)], x_r.at[q])
-        s = xbuf[q, 0]
-        for i in range(1, nx):
-            s = s + xbuf[q, i]
+        spread(q, 0, band, v)
+
+    def second_phase(q):
+        s = collect(q, 0)
         xsum[q] = s
-        for i in sorted(range(1, ny), key=lambda i: -min(i, ny - i)):
-            y_copy(q, i).start()
-        ybuf[q, y] = s
-
-    def mom_copy(q):
-        return pltpu.make_async_copy(movm.at[q], mom_out.at[q], loc.at[5])
-
-    def upd_copy(q):
-        return pltpu.make_async_copy(updv.at[q], upd_out.at[q], loc.at[6])
+        spread(q, 1, xsum, s)
 
     def keep(q):
-        movm[q] = g[q] + product(q, ng - 1) - lift(q, band[q])
-        mom_copy(q).start()
+        mom_out[q] = g[q] + far_part(q) - lift(q, band[q])
 
     def finish(q):
-        if ny > 1:
-            drain(ybuf.at[q, pl.ds(0, ny - 1)], y_r.at[q])
-        s = ybuf[q, 0]
-        for i in range(1, ny):
-            s = s + ybuf[q, i]
-        updv[q] = lift(q, s).astype(bf16)
-        upd_copy(q).start()
+        upd_out[q] = lift(q, collect(q, 1)).astype(bf16)
 
     def arrive(q, h):
         if h < ng - 1:
@@ -257,25 +282,30 @@
             hand(q, h, 1, here).start()
 
     def gather(q, h):
-        drain(o.at[q, h, pl.ds(2 * td, 2 * td)], part_r.at[q, h])
         if h < ng - 1:
-            g[q] += product(q, h)
+            drain(o.at[q, h, pl.ds(2 * td, 2 * td)], part_r.at[q, h])
+            g[q] += mm(ht[h, :, pl.ds(0, 4 * td)], o[q, h, pl.ds(0, 4 * td)])
             if h == ng - 2:
                 partial(q)
+        else:
+            drain(slot(q, h, 3), part_r.at[q, h])
 
     for c in consts:
         c.wait()
-    turn(0)
+    turn(ng - 1)
     drain(g, loc.at[4])
+    drain(o.at[:, ng - 1, pl.ds(0, td)], loc.at[3])
     for q in range(NQ):
+        drain(slot(q, ng - 1, 2), loc.at[5 + ng + q])
         g[q] = 0.9 * g[q]
+        near_part(q)
         if ng == 1:
             bases(q)
             partial(q)
-    drain(o.at[:, ng - 1, pl.ds(0, td)], loc.at[3])
-
-    extra = [functools.partial(turn, gi) for gi in range(1, ng)]
+
+    extra = [functools.partial(turn, gi) for gi in range(1, ng - 1)]
     if ng > 1:
+        turn(0)
         extra += [functools.partial(bases, q) for q in range(NQ)]
     prior = None
     for h in range(ng):
@@ -289,19 +319,16 @@
             if prior is not None:
                 gather(*prior)
                 if prior[1] == ng - 1:
-                    x_send(prior[0])
-                    if prior[0] >= 2:
-                        y_send(prior[0] - 2)
+                    first_phase(prior[0])
             prior = (q, h)
     gather(*prior)
-    x_send(NQ - 1)
-    y_send(NQ - 3)
-    y_send(NQ - 2)
+    first_phase(NQ - 1)
     keep(0)
-    y_send(NQ - 1)
+    for q in SECOND:
+        second_phase(q)
     for q in range(1, NQ):
         keep(q)
-    for q in range(NQ):
+    for q in LAST:
         finish(q)
     if ng > 1:
         drain(o.at[:, pl.ds(0, ng - 1), pl.ds(0, 2 * td)], send_s.at[0])
@@ -314,8 +341,6 @@
         drain(xbuf.at[:, pl.ds(0, nx - 1)], send_s.at[4])
     if ny > 1:
         drain(ybuf.at[:, pl.ds(0, ny - 1)], send_s.at[5])
-    drain(movm, loc.at[5])
-    drain(updv, loc.at[6])
 
 
 def out_kernel(mom_in, upd_in, mom_out, upd_out, sems):
@@ -338,8 +363,10 @@
     ng = nz // 2
     dma = pltpu.SemaphoreType.DMA
     n_greet = max(1, (nx // 2 - 1 if nx > 1 else 0) + (ny // 2 - 1 if ny > 1 else 0))
+    rows_all = 4 * td + 2 * (-2 * td % 128)
     anyspace = pl.BlockSpec(memory_space=pl.ANY)
     hbm = pl.BlockSpec(memory_space=pltpu.HBM)
+    vmem = pl.BlockSpec(memory_space=pltpu.VMEM)
     step = pl.pallas_call(
         functools.partial(kernel, dims, td),
         name="demo_step",
@@ -348,23 +375,22 @@
             jax.ShapeDtypeStruct((NQ, 256, QW), bf16),
         ),
         in_specs=[hbm] * 6,
-        out_specs=(anyspace, anyspace),
+        out_specs=(vmem, vmem),
         scratch_shapes=[
-            pltpu.VMEM((ng, 4 * td, 256), bf16),
-            pltpu.VMEM((ng, 256, 4 * td), bf16),
-            pltpu.VMEM((NQ, ng, 4 * td, QW), bf16),
+            pltpu.VMEM((ng, rows_all, 256), bf16),
+            pltpu.VMEM((ng, 256, rows_all), bf16),
+            pltpu.VMEM((NQ, ng, rows_all, QW), bf16),
             pltpu.VMEM((NQ, 256, QW), f32),
             pltpu.VMEM((NQ, 2, 128, 256), bf16),
-            pltpu.VMEM((NQ, 2, 256, 128), bf16),
-            pltpu.VMEM((NQ, 2, 128, 512), bf16),
-            pltpu.VMEM((NQ, 2, 128, 4 * td), bf16),
+            pltpu.VMEM((NQ, 256, 384), bf16),
+            pltpu.VMEM((NQ, 128, 384), bf16),
+            pltpu.VMEM((NQ, 384, 128), bf16),
+            pltpu.VMEM((NQ, 256, 2 * td), bf16),
             pltpu.VMEM((NQ, 128, 128), f32),
             pltpu.VMEM((NQ, 16, 128), f32),
             pltpu.VMEM((NQ, nx, 16, 128), f32),
             pltpu.VMEM((NQ, 16, 128), f32),
             pltpu.VMEM((NQ, ny, 16, 128), f32),
-            pltpu.VMEM((NQ, 256, QW), f32),
-            pltpu.VMEM((NQ, 256, QW), bf16),
             pltpu.VMEM((256, 256), f32),
             pltpu.SMEM((4, 8), jnp.int32),
             pltpu.SMEM((4, 8), jnp.int32),
@@ -373,7 +399,7 @@
             dma((NQ, ng)),
             dma((NQ,)),
             dma((NQ,)),
-            dma((7 + ng,)),
+            dma((5 + ng + NQ,)),
             pltpu.SemaphoreType.REGULAR((n_greet,)),
         ],
         compiler_params=pltpu.CompilerParams(

time: 51.7 us -> 50.6 us (0.979)
  Pallas kernels: 50.9 us -> 49.9 us
    pallas_call x1, Pallas kernels: 50 us -> 48.9 us  [build(): step(*[pltpu.with_memory_space_constraint(a, pltpu.HBM) for a in args])]
where the time goes in v3:
time: 50.6 us; the launch traced here: 50.5 us
  Pallas kernels  49.9 us (99%)
  between operations  0.64 us (1%)
    pallas_call x1, Pallas kernels, build(): step(*[pltpu.with_memory_space_constraint(a, pltpu.HBM) for a in args])  48.9 us

profile of v3, /device:TPU:1, one launch (start us, length us, event | category | flops | bytes accessed | tf_op | source)
XLA Modules:
  0.0 50.5 jit_solution(508946769416702706)
XLA Ops:
  0.6 48.9 %demo_step.1 = (f32[4,256,128]{2,1,0:T(8,128)S(1)}, bf16[4,256,128]{2,1,0:T(8,128)(2,1)S(1)}) custom-call(bf16[288,512]{1,0:T(8,128)(2,1)} %og.1, bf16[4608,256]{1,0:T(8,128)(2,1)} %hid.1, f32[1,256,512]{2,1,0:T(8,128)} %mom.1, s32[4,8]{1,0:T(4,128)} %rows_any.1, s32[4,8]{1,0:T(4,128)} %cols_any.1, f32[256,256]{1,0:T(8,128)} %constant.2.clone.dmat_any), custom_call_target="tpu_custom_call" | custom-call | tf_op jit(solution)/shard_map/demo_step/pallas_call | solution.py:421
  49.6 0.9 %results_out.1 = (f32[1,256,512]{2,1,0:T(8,128)}, bf16[256,512]{1,0:T(8,128)(2,1)}) custom-call(f32[4,256,128]{2,1,0:T(8,128)S(1)} %get-tuple-element.4.mom_in, bf16[4,256,128]{2,1,0:T(8,128)(2,1)S(1)} %get-tuple-element.5.upd_in), custom_call_target="tpu_custom_call" | custom-call | tf_op jit(solution)/shard_map/results_out/pallas_call | solution.py:421

commit v4 on v3

--- a/solution.py
+++ b/solution.py
@@ -12,6 +12,7 @@
 NX = 4
 NQ = 4
 QW = 128
+PARTS = 4
 Y_FIRST = (0, 1)
 SECOND = (2, 3, 0, 1)
 LAST = (0, 1, 2, 3)
@@ -131,7 +132,7 @@
 
     def hand(q, gi, k, src):
         own = gi == ng - 1 and k == 0
-        return remote(src, slot(q, gi, k + 2), send_s.at[3], loc.at[5 + ng + q] if own else part_r.at[q, gi], partner)
+        return remote(src, slot(q, gi, k + 2), send_s.at[3], loc.at[5 + ng] if own else part_r.at[q, gi], partner)
 
     def send_far(q, sources):
         for side, go in enumerate((go_right, go_left)):
@@ -261,10 +262,10 @@
         spread(q, 1, xsum, s)
 
     def keep(q):
-        mom_out[q] = g[q] + far_part(q) - lift(q, band[q])
+        mom_out[0, :, pl.ds(q * QW, QW)] = g[q] + far_part(q) - lift(q, band[q])
 
     def finish(q):
-        upd_out[q] = lift(q, collect(q, 1)).astype(bf16)
+        upd_out[:, pl.ds(q * QW, QW)] = lift(q, collect(q, 1)).astype(bf16)
 
     def arrive(q, h):
         if h < ng - 1:
@@ -295,8 +296,8 @@
     turn(ng - 1)
     drain(g, loc.at[4])
     drain(o.at[:, ng - 1, pl.ds(0, td)], loc.at[3])
+    drain(o.at[:, ng - 1, pl.ds(0, td)], loc.at[5 + ng])
     for q in range(NQ):
-        drain(slot(q, ng - 1, 2), loc.at[5 + ng + q])
         g[q] = 0.9 * g[q]
         near_part(q)
         if ng == 1:
@@ -344,17 +345,18 @@
 
 
 def out_kernel(mom_in, upd_in, mom_out, upd_out, sems):
-    def copies(q):
+    def copies(k):
+        part = pl.ds(k * (256 // PARTS), 256 // PARTS)
         return (
-            pltpu.make_async_copy(mom_in.at[q], mom_out.at[0, :, pl.ds(q * QW, QW)], sems.at[0, q]),
-            pltpu.make_async_copy(upd_in.at[q], upd_out.at[:, pl.ds(q * QW, QW)], sems.at[1, q]),
+            pltpu.make_async_copy(mom_in.at[0, part], mom_out.at[0, part], sems.at[0, k]),
+            pltpu.make_async_copy(upd_in.at[part], upd_out.at[part], sems.at[1, k]),
         )
 
-    for q in range(NQ):
-        for c in copies(q):
+    for k in range(PARTS):
+        for c in copies(k):
             c.start()
-    for q in range(NQ):
-        for c in copies(q):
+    for k in range(PARTS):
+        for c in copies(k):
             c.wait()
 
 
@@ -371,8 +373,8 @@
         functools.partial(kernel, dims, td),
         name="demo_step",
         out_shape=(
-            jax.ShapeDtypeStruct((NQ, 256, QW), f32),
-            jax.ShapeDtypeStruct((NQ, 256, QW), bf16),
+            jax.ShapeDtypeStruct((1, 256, 512), f32),
+            jax.ShapeDtypeStruct((256, 512), bf16),
         ),
         in_specs=[hbm] * 6,
         out_specs=(vmem, vmem),
@@ -399,7 +401,7 @@
             dma((NQ, ng)),
             dma((NQ,)),
             dma((NQ,)),
-            dma((5 + ng + NQ,)),
+            dma((6 + ng,)),
             pltpu.SemaphoreType.REGULAR((n_greet,)),
         ],
         compiler_params=pltpu.CompilerParams(
@@ -415,7 +417,7 @@
         ),
         in_specs=[anyspace, anyspace],
         out_specs=(anyspace, anyspace),
-        scratch_shapes=[dma((2, NQ))],
+        scratch_shapes=[dma((2, PARTS))],
         compiler_params=pltpu.CompilerParams(vmem_limit_bytes=2**20),
     )
     return lambda *args: out(*step(*[pltpu.with_memory_space_constraint(a, pltpu.HBM) for a in args]))

time: 50.6 us -> 50.3 us (level)
  no operation moved by 1% of the time
where the time goes in v4:
time: 50.3 us; the launch traced here: 50.2 us
  Pallas kernels  49.5 us (98%)
  between operations  0.64 us (1%)
    pallas_call x1, Pallas kernels, build(): step(*[pltpu.with_memory_space_constraint(a, pltpu.HBM) for a in args])  48.6 us

profile of v4, /device:TPU:1, one launch (start us, length us, event | category | flops | bytes accessed | tf_op | source)
XLA Modules:
  0.0 50.2 jit_solution(7282528287689592522)
XLA Ops:
  0.6 48.6 %demo_step.1 = (f32[1,256,512]{2,1,0:T(8,128)S(1)}, bf16[256,512]{1,0:T(8,128)(2,1)S(1)}) custom-call(bf16[288,512]{1,0:T(8,128)(2,1)} %og.1, bf16[4608,256]{1,0:T(8,128)(2,1)} %hid.1, f32[1,256,512]{2,1,0:T(8,128)} %mom.1, s32[4,8]{1,0:T(4,128)} %rows_any.1, s32[4,8]{1,0:T(4,128)} %cols_any.1, f32[256,256]{1,0:T(8,128)} %constant.2.clone.dmat_any), custom_call_target="tpu_custom_call" | custom-call | tf_op jit(solution)/shard_map/demo_step/pallas_call | solution.py:423
  49.2 0.9 %results_out.1 = (f32[1,256,512]{2,1,0:T(8,128)}, bf16[256,512]{1,0:T(8,128)(2,1)}) custom-call(f32[1,256,512]{2,1,0:T(8,128)S(1)} %get-tuple-element.4.mom_in, bf16[256,512]{1,0:T(8,128)(2,1)S(1)} %get-tuple-element.5.upd_in), custom_call_target="tpu_custom_call" | custom-call | tf_op jit(solution)/shard_map/results_out/pallas_call | solution.py:423

commit v5 on v4

--- a/solution.py
+++ b/solution.py
@@ -13,8 +13,8 @@
 NQ = 4
 QW = 128
 PARTS = 4
-Y_FIRST = (0, 1)
-SECOND = (2, 3, 0, 1)
+Y_FIRST = (0, 2)
+SECOND = (1, 0, 3, 2)
 LAST = (0, 1, 2, 3)
 f32 = jnp.float32
 bf16 = jnp.bfloat16

time: 50.3 us -> 50.5 us (level)
  no operation moved by 1% of the time
where the time goes in v5:
time: 50.5 us; the launch traced here: 50.4 us
  Pallas kernels  49.8 us (99%)
  between operations  0.64 us (1%)
    pallas_call x1, Pallas kernels, build(): step(*[pltpu.with_memory_space_constraint(a, pltpu.HBM) for a in args])  48.8 us

profile of v5, /device:TPU:1, one launch (start us, length us, event | category | flops | bytes accessed | tf_op | source)
XLA Modules:
  0.0 50.4 jit_solution(17707610848525818425)
XLA Ops:
  0.6 48.8 %demo_step.1 = (f32[1,256,512]{2,1,0:T(8,128)S(1)}, bf16[256,512]{1,0:T(8,128)(2,1)S(1)}) custom-call(bf16[288,512]{1,0:T(8,128)(2,1)} %og.1, bf16[4608,256]{1,0:T(8,128)(2,1)} %hid.1, f32[1,256,512]{2,1,0:T(8,128)} %mom.1, s32[4,8]{1,0:T(4,128)} %rows_any.1, s32[4,8]{1,0:T(4,128)} %cols_any.1, f32[256,256]{1,0:T(8,128)} %constant.2.clone.dmat_any), custom_call_target="tpu_custom_call" | custom-call | tf_op jit(solution)/shard_map/demo_step/pallas_call | solution.py:423
  49.5 0.9 %results_out.1 = (f32[1,256,512]{2,1,0:T(8,128)}, bf16[256,512]{1,0:T(8,128)(2,1)}) custom-call(f32[1,256,512]{2,1,0:T(8,128)S(1)} %get-tuple-element.4.mom_in, bf16[256,512]{1,0:T(8,128)(2,1)S(1)} %get-tuple-element.5.upd_in), custom_call_target="tpu_custom_call" | custom-call | tf_op jit(solution)/shard_map/results_out/pallas_call | solution.py:423
